TPU v7x, 32 devices: a whole 2x2x4 slice. The times are simulated.
32 devices in a mesh: grp: 4 (over y, x), row: 8 (over z, core).
Axes of the slice: x: 2, y: 2, z: 4, core: 2. Of those that a mesh axis runs over, the one named last changes fastest.
Arguments:
- matrix_tiles: float32 [128, 32, 128, 128], P(('grp', 'row')), may hold values from -2 to 2, as said below
- column_index: int32 [128, 32], P(('grp', 'row')), may hold values from 0 to 127, as said below
- precond: float32 [128, 128, 128], P(('grp', 'row')), may hold values from -12 to 16, as said below
- right_side: float32 [128, 16, 128], P(('grp', 'row')), may hold values from -60 to 60
- lost_group: int32 [1], replicated, may hold values from 0 to 16383
Outputs:
- recovered: float32 [128, 16, 128], P(('grp', 'row'))
- true_residual: float32 [128, 16, 128], P(('grp', 'row'))
Inputs may be any that keep to these rules, and one draw needn't show every extreme that they name: `column_index`: entry 0 of block row i is i; entry 1 is i + 12, or i - 12 where i + 12 passes the end; every entry lies within 12 of its block row. `precond`: every block is symmetric positive definite. `matrix_tiles`: the diagonal tile of each block row is near the identity.
All inputs are finite; a program needn't handle non-finite values.
Results may differ from a plain program's by a relative error of at most 0.0003.
Values sent between devices are 32-bit elements; how exact they have to be, the bound alone decides.
No kernel may reach another device: no remote copies, remote signals or barrier semaphores. Data moves between devices by JAX's collectives and lax.ppermute only.
A program may use at most 64 MiB of HBM per device.

v0:
```python
import jax
import jax.numpy as jnp
from jax import lax
from jax.sharding import PartitionSpec as P

REACH = 3
OUTER = 2
INNER = 2
BAND = 12


def from_behind(value, axis, steps):
    count = lax.axis_size(axis)
    first, last = (max(0, -steps), min(count, count - steps))
    return lax.ppermute(value, axis, [(source, source + steps) for source in range(first, last)])


def inner_products(former, latter):
    return jnp.einsum("ica,ida->cd", former, latter, precision=lax.Precision.HIGHEST)


def scaled_by(vector, coeffs):
    return jnp.einsum("ica,cd->ida", vector, coeffs, precision=lax.Precision.HIGHEST)


def small_product(former, latter):
    return jnp.dot(former, latter, precision=lax.Precision.HIGHEST)


def solve_sym(matrix, target):
    factor = jnp.linalg.cholesky(0.5 * (matrix + matrix.T))
    middle = lax.linalg.triangular_solve(factor, target, left_side=True, lower=True)
    return lax.linalg.triangular_solve(factor, middle, left_side=True, lower=True, transpose_a=True)


def neighbour(vector, offset):
    return from_behind(vector, ("grp", "row"), offset)


def group_neighbour(vector, offset):
    return from_behind(vector, "row", offset)


def window_of(vector, shifter):
    pieces = [shifter(vector, offset) for offset in range(REACH, 0, -1)]
    pieces.append(vector)
    for offset in range(1, REACH + 1):
        pieces.append(shifter(vector, -offset))
    return jnp.concatenate(pieces, 0)


def tile_product(matrix_tiles, window, local_cols, kept_mask):
    picked = jnp.take(window, local_cols, axis=0)
    if kept_mask is not None:
        picked = picked * kept_mask[:, :, None, None]
    return jnp.einsum("ikab,ikcb->ica", matrix_tiles, picked, precision=lax.Precision.HIGHEST)


def per_device(matrix_tiles, column_index, precond, right_side, lost_group):
    blocks = right_side.shape[0]
    row_count = lax.axis_size("row")
    group_count = lax.axis_size("grp")
    group_blocks = blocks * row_count
    my_group = lax.axis_index("grp")
    my_start = lax.axis_index(("grp", "row")) * blocks
    local_cols = column_index - (my_start - BAND)
    other_mask = (column_index // group_blocks != my_group).astype(jnp.float32)
    own_mask = 1.0 - other_mask
    lost = lost_group[0] % group_count

    def full_product(vector):
        return tile_product(matrix_tiles, window_of(vector, neighbour), local_cols, None)

    solution = jnp.zeros_like(right_side)
    residual = right_side
    direction = right_side
    squares = lax.psum(inner_products(residual, residual), ("grp", "row"))
    for outer_step in range(OUTER):
        applied = full_product(direction)
        curvature, crossed, square = lax.psum(
            (
                inner_products(direction, applied),
                inner_products(applied, residual),
                inner_products(applied, applied),
            ),
            ("grp", "row"),
        )
        advance = solve_sym(curvature, squares)
        solution = solution + scaled_by(direction, advance)
        residual = residual - scaled_by(applied, advance)
        squares_next = (
            squares
            - small_product(crossed.T, advance)
            - small_product(advance.T, crossed)
            + small_product(advance.T, small_product(square, advance))
        )
        mixing = solve_sym(squares, squares_next)
        direction = residual + scaled_by(direction, mixing)
        squares = squares_next
    coupled = tile_product(matrix_tiles, window_of(solution, neighbour), local_cols, other_mask)
    inner_target = right_side - coupled

    def condition(vector):
        return jnp.einsum("iab,icb->ica", precond, vector, precision=lax.Precision.HIGHEST)

    estimate = jnp.zeros_like(inner_target)
    remainder = inner_target
    smoothed = condition(remainder)
    heading = smoothed
    weight = lax.psum(inner_products(remainder, smoothed), "row")
    for inner_step in range(INNER):
        applied = tile_product(
            matrix_tiles, window_of(heading, group_neighbour), local_cols, own_mask
        )
        bending = lax.psum(inner_products(heading, applied), "row")
        advance = solve_sym(bending, weight)
        estimate = estimate + scaled_by(heading, advance)
        remainder = remainder - scaled_by(applied, advance)
        if inner_step + 1 < INNER:
            smoothed = condition(remainder)
            weight_next = lax.psum(inner_products(remainder, smoothed), "row")
            heading = smoothed + scaled_by(heading, solve_sym(weight, weight_next))
            weight = weight_next
    recovered = jnp.where(my_group == lost, estimate, solution)
    true_residual = right_side - full_product(recovered)
    return (recovered, true_residual)


def solution(mesh):
    in_specs = (
        P(("grp", "row"), None, None, None),
        P(("grp", "row"), None),
        P(("grp", "row"), None, None),
        P(("grp", "row"), None, None),
        P(),
    )
    out_specs = (P(("grp", "row"), None, None), P(("grp", "row"), None, None))
    return jax.shard_map(
        per_device, mesh=mesh, in_specs=in_specs, out_specs=out_specs, check_vma=False
    )
```

profile of v0, /device:TPU:5, one launch (start us, length us, event | category | flops | bytes accessed | tf_op | source)
XLA Modules:
  0.0 370.1 jit_solution(12967061510973747642)
XLA Ops:
  0.6 6.8 %collective-permute-start.5 = (f32[4,16,128]{2,1,0:T(8,128)}, f32[4,16,128]{2,1,0:T(8,128)S(1)}, u32[]{:S(2)}, u32[]{:S(2)}) collective-permute-start(f32[4,16,128]{2,1,0:T(8,128)} %param.15), channel_id=1, source_target_pairs={{3,0},{4,1},{5,2},{6,3},{7,4},{8,5},{9,6},{10,7},{11,8},{12,9},{13... | collective-permute-start | bytes 98312 | tf_op jit(solution)/shard_map/ppermute | solution.py:15
  7.4 2.1 collective-permute-start.4
  9.5 2.1 collective-permute-start.3
  11.7 3.4 collective-permute-start.2
  15.1 2.9 collective-permute-start
  19.8 4.3 %collective-permute-done = f32[4,16,128]{2,1,0:T(8,128)S(1)} collective-permute-done((f32[4,16,128]{2,1,0:T(8,128)}, f32[4,16,128]{2,1,0:T(8,128)S(1)}, u32[]{:S(2)}, u32[]{:S(2)}) %collective-permute-start) | collective-permute-done | bytes 32800 | tf_op jit(solution)/shard_map/ppermute | solution.py:15
  24.2 1.9 collective-permute-start.1
  26.1 6.5 %collective-permute-done.1 = f32[4,16,128]{2,1,0:T(8,128)S(1)} collective-permute-done((f32[4,16,128]{2,1,0:T(8,128)}, f32[4,16,128]{2,1,0:T(8,128)S(1)}, u32[]{:S(2)}, u32[]{:S(2)}) %collective-permute-start.1) | collective-permute-done | bytes 32800 | tf_op jit(solution)/shard_map/ppermute | solution.py:15
  34.2 9.4 %convolution_bitcast_fusion.9 = f32[4,16,128]{2,1,0:T(8,128)S(1)} fusion(f32[4,32,128,128]{3,2,1,0:T(8,128)} %param.12, f32[4,32,16,128]{3,2,1,0:T(8,128)S(1)} %bitcast.254, pred[4,32]{1,0:T(4,128)(4,1)S(1)} %get-tuple-element.14), kind=kOutput, calls=%fused_computation.26 | convolution fusion | flops 402915328 | bytes 9470080 | tf_op jit(solution)/shard_map/ikab,ikcb->ica/dot_general | solution.py:56
  44.0 36.1 %all-reduce = (f32[16,16]{1,0:T(8,128)S(1)}, f32[16,16]{1,0:T(8,128)S(1)}, f32[16,16]{1,0:T(8,128)S(1)}, f32[16,16]{1,0:T(8,128)S(1)}) all-reduce(f32[16,16]{1,0:T(8,128)S(1)} %convolution_bitcast_fusion.21, f32[16,16]{1,0:T(8,128)S(1)} %bitcast.256, ...), channel_id=1, replica_groups=mesh['grp'=4,'row'=8] {'grp','row'}, use_global_device_ids=true, to_apply=%region_3.6 | all-reduce | flops 1024 | bytes 8192 | tf_op jit(solution)/shard_map/psum | solution.py:77
  80.3 1.5 cholesky.115
  83.1 1.2 custom-call.21
  84.4 1.5 cholesky.104
  87.2 1.2 custom-call.19
  90.4 6.3 %collective-permute-start.6 = (f32[4,16,128]{2,1,0:T(8,128)S(1)}, f32[4,16,128]{2,1,0:T(8,128)S(1)}, u32[]{:S(2)}, u32[]{:S(2)}) collective-permute-start(f32[4,16,128]{2,1,0:T(8,128)S(1)} %fusion.7), channel_id=1, source_target_pairs={{0,3},{1,4},{2,5},{3,6},{4,7},{5,8},{6,9},{7,10},{8,11},{9,12},{10... | collective-permute-start | bytes 98312 | tf_op jit(solution)/shard_map/ppermute | solution.py:15
  96.9 2.8 collective-permute-start.11
  99.8 4.8 %collective-permute-start.10 = (f32[4,16,128]{2,1,0:T(8,128)S(1)}, f32[4,16,128]{2,1,0:T(8,128)S(1)}, u32[]{:S(2)}, u32[]{:S(2)}) collective-permute-start(f32[4,16,128]{2,1,0:T(8,128)S(1)} %fusion.7), channel_id=1, source_target_pairs={{2,0},{3,1},{4,2},{5,3},{6,4},{7,5},{8,6},{9,7},{10,8},{11,9},{12,... | collective-permute-start | bytes 98312 | tf_op jit(solution)/shard_map/ppermute | solution.py:15
  104.6 1.9 collective-permute-start.9
  106.5 3.6 collective-permute-start.8
  110.2 2.5 collective-permute-start.7
  112.7 5.8 %collective-permute-done.7 = f32[4,16,128]{2,1,0:T(8,128)S(1)} collective-permute-done((f32[4,16,128]{2,1,0:T(8,128)S(1)}, f32[4,16,128]{2,1,0:T(8,128)S(1)}, u32[]{:S(2)}, u32[]{:S(2)}) %collective-permute-start.7) | collective-permute-done | bytes 32800 | tf_op jit(solution)/shard_map/ppermute | solution.py:15
  119.3 9.4 %convolution_bitcast_fusion.6 = f32[4,16,128]{2,1,0:T(8,128)S(1)} fusion(f32[4,32,128,128]{3,2,1,0:T(8,128)} %param.12, f32[4,32,16,128]{3,2,1,0:T(8,128)S(1)} %bitcast.255, pred[4,32]{1,0:T(4,128)(4,1)S(1)} %get-tuple-element.14), kind=kOutput, calls=%fused_computation.21 | convolution fusion | flops 402915328 | bytes 9470080 | tf_op jit(solution)/shard_map/ikab,ikcb->ica/dot_general | solution.py:56
  128.8 36.1 %psum.67 = f32[16,16]{1,0:T(8,128)S(1)} all-reduce(f32[16,16]{1,0:T(8,128)S(1)} %convolution_bitcast_fusion.18), channel_id=1, replica_groups=mesh['grp'=4,'row'=8] {'grp','row'}, use_global_device_ids=true, to_apply=%region_6.11 | all-reduce | flops 256 | bytes 2048 | tf_op jit(solution)/shard_map/psum | solution.py:80
  165.1 1.5 cholesky.126
  167.9 1.2 custom-call.23
  169.7 6.0 %collective-permute-start.12 = (f32[4,16,128]{2,1,0:T(8,128)S(1)}, f32[4,16,128]{2,1,0:T(8,128)S(1)}, u32[]{:S(2)}, u32[]{:S(2)}) collective-permute-start(f32[4,16,128]{2,1,0:T(8,128)S(1)} %fusion.6), channel_id=1, source_target_pairs={{0,3},{1,4},{2,5},{3,6},{4,7},{5,8},{6,9},{7,10},{8,11},{9,12},{10... | collective-permute-start | bytes 98312 | tf_op jit(solution)/shard_map/ppermute | solution.py:15
  176.4 3.2 collective-permute-start.17
  179.6 4.4 %collective-permute-start.16 = (f32[4,16,128]{2,1,0:T(8,128)S(1)}, f32[4,16,128]{2,1,0:T(8,128)S(1)}, u32[]{:S(2)}, u32[]{:S(2)}) collective-permute-start(f32[4,16,128]{2,1,0:T(8,128)S(1)} %fusion.6), channel_id=1, source_target_pairs={{2,0},{3,1},{4,2},{5,3},{6,4},{7,5},{8,6},{9,7},{10,8},{11,9},{12,... | collective-permute-start | bytes 98312 | tf_op jit(solution)/shard_map/ppermute | solution.py:15
  184.0 1.9 collective-permute-start.15
  186.0 3.6 collective-permute-start.14
  189.6 2.7 collective-permute-start.13
  192.3 5.6 %collective-permute-done.13 = f32[4,16,128]{2,1,0:T(8,128)S(1)} collective-permute-done((f32[4,16,128]{2,1,0:T(8,128)S(1)}, f32[4,16,128]{2,1,0:T(8,128)S(1)}, u32[]{:S(2)}, u32[]{:S(2)}) %collective-permute-start.13) | collective-permute-done | bytes 32800 | tf_op jit(solution)/shard_map/ppermute | solution.py:15
  198.8 9.4 %fusion.5 = f32[4,16,128]{2,1,0:T(8,128)S(1)} fusion(f32[4,16,128]{2,1,0:T(8,128)S(1)} %copy-done.1, f32[4,32,128,128]{3,2,1,0:T(8,128)} %param.12, f32[4,32,16,128]{3,2,1,0:T(8,128)S(1)} %bitcast.250, f32[4,32]{1,0:T(4,128)S(1)} %get-tuple-element.13, pred[4,32]{1,0:T(4,128)(4,1)S(1)} %get-tuple-element.14), kind=kOutput, calls=%fused_computation.18 | convolution fusion | flops 403185664 | bytes 9503360 | tf_op jit(solution)/shard_map/ikab,ikcb->ica/dot_general | solution.py:56
  208.7 1.3 collective-permute-start.18
  210.2 1.3 collective-permute-start.23
  211.5 1.3 collective-permute-start.22
  212.8 1.9 collective-permute-start.21
  214.7 4.1 %collective-permute-start.20 = (f32[4,16,128]{2,1,0:T(8,128)S(1)}, f32[4,16,128]{2,1,0:T(8,128)S(1)}, u32[]{:S(2)}, u32[]{:S(2)}) collective-permute-start(f32[4,16,128]{2,1,0:T(8,128)S(1)} %fusion.85), channel_id=1, source_target_pairs={{0,1},{1,2},{2,3},{3,4},{4,5},{5,6},{6,7},{8,9},{9,10},{10,11},{11... | collective-permute-start | bytes 98312 | tf_op jit(solution)/shard_map/ppermute | solution.py:15
  218.8 4.0 %collective-permute-start.19 = (f32[4,16,128]{2,1,0:T(8,128)S(1)}, f32[4,16,128]{2,1,0:T(8,128)S(1)}, u32[]{:S(2)}, u32[]{:S(2)}) collective-permute-start(f32[4,16,128]{2,1,0:T(8,128)S(1)} %fusion.85), channel_id=1, source_target_pairs={{0,2},{1,3},{2,4},{3,5},{4,6},{5,7},{8,10},{9,11},{10,12},{11,13},... | collective-permute-start | bytes 98312 | tf_op jit(solution)/shard_map/ppermute | solution.py:15
  224.7 9.4 %convolution_bitcast_fusion.4 = f32[4,16,128]{2,1,0:T(8,128)S(1)} fusion(f32[4,32,128,128]{3,2,1,0:T(8,128)} %param.12, f32[4,32,16,128]{3,2,1,0:T(8,128)S(1)} %bitcast.251, f32[4,32]{1,0:T(4,128)S(1)} %get-tuple-element.12, pred[4,32]{1,0:T(4,128)(4,1)S(1)} %get-tuple-element.14), kind=kOutput, calls=%fused_computation.16 | convolution fusion | flops 403177472 | bytes 9470592 | tf_op jit(solution)/shard_map/ikab,ikcb->ica/dot_general | solution.py:56
  234.2 24.9 %all-reduce.1 = (f32[16,16]{1,0:T(8,128)S(1)}, f32[16,16]{1,0:T(8,128)S(1)}) all-reduce(f32[16,16]{1,0:T(8,128)S(1)} %convolution_bitcast_fusion.15, f32[16,16]{1,0:T(8,128)S(1)} %convolution_bitcast_fusion.16), channel_id=1, replica_groups=mesh['grp'=4,'row'=8] {'row'}, use_global_device_ids=true, to_apply=%region_8.13 | all-reduce | flops 512 | bytes 4096 | tf_op jit(solution)/shard_map/psum | solution.py:110
  259.3 1.5 cholesky.137
  262.1 1.2 custom-call.25
  264.1 1.5 cholesky.148
  266.9 1.2 custom-call.27
  268.8 17.3 %psum.70 = f32[16,16]{1,0:T(8,128)S(1)} all-reduce(f32[16,16]{1,0:T(8,128)S(1)} %convolution_bitcast_fusion.13), channel_id=1, replica_groups=mesh['grp'=4,'row'=8] {'row'}, use_global_device_ids=true, to_apply=%region_9.14 | all-reduce | flops 256 | bytes 2048 | tf_op jit(solution)/shard_map/psum | solution.py:121
  286.6 1.3 collective-permute-start.24
  288.1 1.3 collective-permute-start.29
  289.4 1.3 collective-permute-start.28
  290.7 2.7 collective-permute-start.27
  293.4 4.2 %collective-permute-start.26 = (f32[4,16,128]{2,1,0:T(8,128)S(1)}, f32[4,16,128]{2,1,0:T(8,128)S(1)}, u32[]{:S(2)}, u32[]{:S(2)}) collective-permute-start(f32[4,16,128]{2,1,0:T(8,128)S(1)} %fusion.3), channel_id=1, source_target_pairs={{0,1},{1,2},{2,3},{3,4},{4,5},{5,6},{6,7},{8,9},{9,10},{10,11},{11... | collective-permute-start | bytes 98312 | tf_op jit(solution)/shard_map/ppermute | solution.py:15
  297.5 4.2 %collective-permute-start.25 = (f32[4,16,128]{2,1,0:T(8,128)S(1)}, f32[4,16,128]{2,1,0:T(8,128)S(1)}, u32[]{:S(2)}, u32[]{:S(2)}) collective-permute-start(f32[4,16,128]{2,1,0:T(8,128)S(1)} %fusion.3), channel_id=1, source_target_pairs={{0,2},{1,3},{2,4},{3,5},{4,6},{5,7},{8,10},{9,11},{10,12},{11,13},... | collective-permute-start | bytes 98312 | tf_op jit(solution)/shard_map/ppermute | solution.py:15
  303.4 9.4 %convolution_bitcast_fusion.1 = f32[4,16,128]{2,1,0:T(8,128)S(1)} fusion(f32[4,32,128,128]{3,2,1,0:T(8,128)} %param.12, f32[4,32,16,128]{3,2,1,0:T(8,128)S(1)} %bitcast.252, f32[4,32]{1,0:T(4,128)S(1)} %get-tuple-element.12, pred[4,32]{1,0:T(4,128)(4,1)S(1)} %get-tuple-element.14), kind=kOutput, calls=%fused_computation.11 | convolution fusion | flops 403177472 | bytes 9470592 | tf_op jit(solution)/shard_map/ikab,ikcb->ica/dot_general | solution.py:56
  313.0 13.9 %psum.71 = f32[16,16]{1,0:T(8,128)S(1)} all-reduce(f32[16,16]{1,0:T(8,128)S(1)} %convolution_bitcast_fusion.11), channel_id=1, replica_groups=mesh['grp'=4,'row'=8] {'row'}, use_global_device_ids=true, to_apply=%region_10.15 | all-reduce | flops 256 | bytes 2048 | tf_op jit(solution)/shard_map/psum | solution.py:115
  327.1 1.5 cholesky.159
  329.9 1.2 custom-call.29
  331.7 1.9 collective-permute-start.30
  333.6 7.2 %collective-permute-start.35 = (f32[4,16,128]{2,1,0:T(8,128)S(1)}, f32[4,16,128]{2,1,0:T(8,128)S(1)}, u32[]{:S(2)}, u32[]{:S(2)}) collective-permute-start(f32[4,16,128]{2,1,0:T(8,128)S(1)} %fusion.2), channel_id=1, source_target_pairs={{3,0},{4,1},{5,2},{6,3},{7,4},{8,5},{9,6},{10,7},{11,8},{12,9},{13... | collective-permute-start | bytes 98312 | tf_op jit(solution)/shard_map/ppermute | solution.py:15
  340.9 1.9 collective-permute-start.34
  342.8 4.0 %collective-permute-start.33 = (f32[4,16,128]{2,1,0:T(8,128)S(1)}, f32[4,16,128]{2,1,0:T(8,128)S(1)}, u32[]{:S(2)}, u32[]{:S(2)}) collective-permute-start(f32[4,16,128]{2,1,0:T(8,128)S(1)} %fusion.2), channel_id=1, source_target_pairs={{1,0},{2,1},{3,2},{4,3},{5,4},{6,5},{7,6},{8,7},{9,8},{10,9},{11,1... | collective-permute-start | bytes 98312 | tf_op jit(solution)/shard_map/ppermute | solution.py:15
  346.8 3.5 collective-permute-start.32
  350.3 2.0 collective-permute-start.31
  352.4 6.8 %collective-permute-done.31 = f32[4,16,128]{2,1,0:T(8,128)S(1)} collective-permute-done((f32[4,16,128]{2,1,0:T(8,128)S(1)}, f32[4,16,128]{2,1,0:T(8,128)S(1)}, u32[]{:S(2)}, u32[]{:S(2)}) %collective-permute-start.31) | collective-permute-done | bytes 32800 | tf_op jit(solution)/shard_map/ppermute | solution.py:15
  360.1 10.0 %fusion = f32[4,16,128]{2,1,0:T(8,128)} fusion(f32[4,16,128]{2,1,0:T(8,128)S(1)} %copy-done.1, f32[4,32,128,128]{3,2,1,0:T(8,128)} %param.12, f32[4,32,16,128]{3,2,1,0:T(8,128)S(1)} %bitcast.253, pred[4,32]{1,0:T(4,128)(4,1)S(1)} %get-tuple-element.14), kind=kOutput, calls=%fused_computation.7 | convolution fusion | flops 402923520 | bytes 9502848 | tf_op jit(solution)/shard_map/ikab,ikcb->ica/dot_general | solution.py:56
  (167 shorter events, 24.8 us)
Async XLA Ops:
  0.6 207.6 %copy-start = (f32[4,128,128]{2,1,0:T(8,128)S(1)}, f32[4,128,128]{2,1,0:T(8,128)}, u32[]{:S(2)}) copy-start(f32[4,128,128]{2,1,0:T(8,128)} %param.14) | copy-start | bytes 786436
  0.6 32.8 %collective-permute-start.5 = (f32[4,16,128]{2,1,0:T(8,128)}, f32[4,16,128]{2,1,0:T(8,128)S(1)}, u32[]{:S(2)}, u32[]{:S(2)}) collective-permute-start(f32[4,16,128]{2,1,0:T(8,128)} %param.15), channel_id=1, source_target_pairs={{3,0},{4,1},{5,2},{6,3},{7,4},{8,5},{9,6},{10,7},{11,8},{12,9},{13... | collective-permute-start | bytes 98312 | tf_op jit(solution)/shard_map/ppermute | solution.py:15
  7.4 26.0 %collective-permute-start.4 = (f32[4,16,128]{2,1,0:T(8,128)}, f32[4,16,128]{2,1,0:T(8,128)S(1)}, u32[]{:S(2)}, u32[]{:S(2)}) collective-permute-start(f32[4,16,128]{2,1,0:T(8,128)} %param.15), channel_id=1, source_target_pairs={{2,0},{3,1},{4,2},{5,3},{6,4},{7,5},{8,6},{9,7},{10,8},{11,9},{12,... | collective-permute-start | bytes 98312 | tf_op jit(solution)/shard_map/ppermute | solution.py:15
  9.5 23.9 %collective-permute-start.3 = (f32[4,16,128]{2,1,0:T(8,128)}, f32[4,16,128]{2,1,0:T(8,128)S(1)}, u32[]{:S(2)}, u32[]{:S(2)}) collective-permute-start(f32[4,16,128]{2,1,0:T(8,128)} %param.15), channel_id=1, source_target_pairs={{1,0},{2,1},{3,2},{4,3},{5,4},{6,5},{7,6},{8,7},{9,8},{10,9},{11,1... | collective-permute-start | bytes 98312 | tf_op jit(solution)/shard_map/ppermute | solution.py:15
  11.7 20.9 %collective-permute-start.2 = (f32[4,16,128]{2,1,0:T(8,128)}, f32[4,16,128]{2,1,0:T(8,128)S(1)}, u32[]{:S(2)}, u32[]{:S(2)}) collective-permute-start(f32[4,16,128]{2,1,0:T(8,128)} %param.15), channel_id=1, source_target_pairs={{0,1},{1,2},{2,3},{3,4},{4,5},{5,6},{6,7},{7,8},{8,9},{9,10},{10,1... | collective-permute-start | bytes 98312 | tf_op jit(solution)/shard_map/ppermute | solution.py:15
  15.1 9.0 %collective-permute-start = (f32[4,16,128]{2,1,0:T(8,128)}, f32[4,16,128]{2,1,0:T(8,128)S(1)}, u32[]{:S(2)}, u32[]{:S(2)}) collective-permute-start(f32[4,16,128]{2,1,0:T(8,128)} %param.15), channel_id=1, source_target_pairs={{0,3},{1,4},{2,5},{3,6},{4,7},{5,8},{6,9},{7,10},{8,11},{9,12},{10... | collective-permute-start | bytes 98312 | tf_op jit(solution)/shard_map/ppermute | solution.py:15
  19.0 24.6 %copy-start.1 = (f32[4,16,128]{2,1,0:T(8,128)S(1)}, f32[4,16,128]{2,1,0:T(8,128)}, u32[]{:S(2)}) copy-start(f32[4,16,128]{2,1,0:T(8,128)} %param.15) | copy-start | bytes 98308
  24.2 8.5 %collective-permute-start.1 = (f32[4,16,128]{2,1,0:T(8,128)}, f32[4,16,128]{2,1,0:T(8,128)S(1)}, u32[]{:S(2)}, u32[]{:S(2)}) collective-permute-start(f32[4,16,128]{2,1,0:T(8,128)} %param.15), channel_id=1, source_target_pairs={{0,2},{1,3},{2,4},{3,5},{4,6},{5,7},{6,8},{7,9},{8,10},{9,11},{10,... | collective-permute-start | bytes 98312 | tf_op jit(solution)/shard_map/ppermute | solution.py:15
  90.4 19.8 %collective-permute-start.6 = (f32[4,16,128]{2,1,0:T(8,128)S(1)}, f32[4,16,128]{2,1,0:T(8,128)S(1)}, u32[]{:S(2)}, u32[]{:S(2)}) collective-permute-start(f32[4,16,128]{2,1,0:T(8,128)S(1)} %fusion.7), channel_id=1, source_target_pairs={{0,3},{1,4},{2,5},{3,6},{4,7},{5,8},{6,9},{7,10},{8,11},{9,12},{10... | collective-permute-start | bytes 98312 | tf_op jit(solution)/shard_map/ppermute | solution.py:15
  96.9 21.6 %collective-permute-start.11 = (f32[4,16,128]{2,1,0:T(8,128)S(1)}, f32[4,16,128]{2,1,0:T(8,128)S(1)}, u32[]{:S(2)}, u32[]{:S(2)}) collective-permute-start(f32[4,16,128]{2,1,0:T(8,128)S(1)} %fusion.7), channel_id=1, source_target_pairs={{3,0},{4,1},{5,2},{6,3},{7,4},{8,5},{9,6},{10,7},{11,8},{12,9},{13... | collective-permute-start | bytes 98312 | tf_op jit(solution)/shard_map/ppermute | solution.py:15
  99.8 18.7 %collective-permute-start.10 = (f32[4,16,128]{2,1,0:T(8,128)S(1)}, f32[4,16,128]{2,1,0:T(8,128)S(1)}, u32[]{:S(2)}, u32[]{:S(2)}) collective-permute-start(f32[4,16,128]{2,1,0:T(8,128)S(1)} %fusion.7), channel_id=1, source_target_pairs={{2,0},{3,1},{4,2},{5,3},{6,4},{7,5},{8,6},{9,7},{10,8},{11,9},{12,... | collective-permute-start | bytes 98312 | tf_op jit(solution)/shard_map/ppermute | solution.py:15
  104.6 13.9 %collective-permute-start.9 = (f32[4,16,128]{2,1,0:T(8,128)S(1)}, f32[4,16,128]{2,1,0:T(8,128)S(1)}, u32[]{:S(2)}, u32[]{:S(2)}) collective-permute-start(f32[4,16,128]{2,1,0:T(8,128)S(1)} %fusion.7), channel_id=1, source_target_pairs={{1,0},{2,1},{3,2},{4,3},{5,4},{6,5},{7,6},{8,7},{9,8},{10,9},{11,1... | collective-permute-start | bytes 98312 | tf_op jit(solution)/shard_map/ppermute | solution.py:15
  106.5 11.9 %collective-permute-start.8 = (f32[4,16,128]{2,1,0:T(8,128)S(1)}, f32[4,16,128]{2,1,0:T(8,128)S(1)}, u32[]{:S(2)}, u32[]{:S(2)}) collective-permute-start(f32[4,16,128]{2,1,0:T(8,128)S(1)} %fusion.7), channel_id=1, source_target_pairs={{0,1},{1,2},{2,3},{3,4},{4,5},{5,6},{6,7},{7,8},{8,9},{9,10},{10,1... | collective-permute-start | bytes 98312 | tf_op jit(solution)/shard_map/ppermute | solution.py:15
  110.2 8.3 %collective-permute-start.7 = (f32[4,16,128]{2,1,0:T(8,128)S(1)}, f32[4,16,128]{2,1,0:T(8,128)S(1)}, u32[]{:S(2)}, u32[]{:S(2)}) collective-permute-start(f32[4,16,128]{2,1,0:T(8,128)S(1)} %fusion.7), channel_id=1, source_target_pairs={{0,2},{1,3},{2,4},{3,5},{4,6},{5,7},{6,8},{7,9},{8,10},{9,11},{10,... | collective-permute-start | bytes 98312 | tf_op jit(solution)/shard_map/ppermute | solution.py:15
  118.5 57.2 %copy-start.3 = (s32[4,32]{1,0:T(4,128)S(1)}, s32[4,32]{1,0:T(4,128)}, u32[]{:S(2)}) copy-start(s32[4,32]{1,0:T(4,128)} %param.13) | copy-start | bytes 1540
  169.7 19.9 %collective-permute-start.12 = (f32[4,16,128]{2,1,0:T(8,128)S(1)}, f32[4,16,128]{2,1,0:T(8,128)S(1)}, u32[]{:S(2)}, u32[]{:S(2)}) collective-permute-start(f32[4,16,128]{2,1,0:T(8,128)S(1)} %fusion.6), channel_id=1, source_target_pairs={{0,3},{1,4},{2,5},{3,6},{4,7},{5,8},{6,9},{7,10},{8,11},{9,12},{10... | collective-permute-start | bytes 98312 | tf_op jit(solution)/shard_map/ppermute | solution.py:15
  176.4 21.6 %collective-permute-start.17 = (f32[4,16,128]{2,1,0:T(8,128)S(1)}, f32[4,16,128]{2,1,0:T(8,128)S(1)}, u32[]{:S(2)}, u32[]{:S(2)}) collective-permute-start(f32[4,16,128]{2,1,0:T(8,128)S(1)} %fusion.6), channel_id=1, source_target_pairs={{3,0},{4,1},{5,2},{6,3},{7,4},{8,5},{9,6},{10,7},{11,8},{12,9},{13... | collective-permute-start | bytes 98312 | tf_op jit(solution)/shard_map/ppermute | solution.py:15
  179.6 18.4 %collective-permute-start.16 = (f32[4,16,128]{2,1,0:T(8,128)S(1)}, f32[4,16,128]{2,1,0:T(8,128)S(1)}, u32[]{:S(2)}, u32[]{:S(2)}) collective-permute-start(f32[4,16,128]{2,1,0:T(8,128)S(1)} %fusion.6), channel_id=1, source_target_pairs={{2,0},{3,1},{4,2},{5,3},{6,4},{7,5},{8,6},{9,7},{10,8},{11,9},{12,... | collective-permute-start | bytes 98312 | tf_op jit(solution)/shard_map/ppermute | solution.py:15
  184.0 13.9 %collective-permute-start.15 = (f32[4,16,128]{2,1,0:T(8,128)S(1)}, f32[4,16,128]{2,1,0:T(8,128)S(1)}, u32[]{:S(2)}, u32[]{:S(2)}) collective-permute-start(f32[4,16,128]{2,1,0:T(8,128)S(1)} %fusion.6), channel_id=1, source_target_pairs={{1,0},{2,1},{3,2},{4,3},{5,4},{6,5},{7,6},{8,7},{9,8},{10,9},{11,1... | collective-permute-start | bytes 98312 | tf_op jit(solution)/shard_map/ppermute | solution.py:15
  186.0 11.9 %collective-permute-start.14 = (f32[4,16,128]{2,1,0:T(8,128)S(1)}, f32[4,16,128]{2,1,0:T(8,128)S(1)}, u32[]{:S(2)}, u32[]{:S(2)}) collective-permute-start(f32[4,16,128]{2,1,0:T(8,128)S(1)} %fusion.6), channel_id=1, source_target_pairs={{0,1},{1,2},{2,3},{3,4},{4,5},{5,6},{6,7},{7,8},{8,9},{9,10},{10,1... | collective-permute-start | bytes 98312 | tf_op jit(solution)/shard_map/ppermute | solution.py:15
  189.6 8.3 %collective-permute-start.13 = (f32[4,16,128]{2,1,0:T(8,128)S(1)}, f32[4,16,128]{2,1,0:T(8,128)S(1)}, u32[]{:S(2)}, u32[]{:S(2)}) collective-permute-start(f32[4,16,128]{2,1,0:T(8,128)S(1)} %fusion.6), channel_id=1, source_target_pairs={{0,2},{1,3},{2,4},{3,5},{4,6},{5,7},{6,8},{7,9},{8,10},{9,11},{10,... | collective-permute-start | bytes 98312 | tf_op jit(solution)/shard_map/ppermute | solution.py:15
  208.7 10.1 %collective-permute-start.18 = (f32[4,16,128]{2,1,0:T(8,128)S(1)}, f32[4,16,128]{2,1,0:T(8,128)S(1)}, u32[]{:S(2)}, u32[]{:S(2)}) collective-permute-start(f32[4,16,128]{2,1,0:T(8,128)S(1)} %fusion.85), channel_id=1, source_target_pairs={{0,3},{1,4},{2,5},{3,6},{4,7},{8,11},{9,12},{10,13},{11,14},{12,15... | collective-permute-start | bytes 98312 | tf_op jit(solution)/shard_map/ppermute | solution.py:15
  210.2 13.7 %collective-permute-start.23 = (f32[4,16,128]{2,1,0:T(8,128)S(1)}, f32[4,16,128]{2,1,0:T(8,128)S(1)}, u32[]{:S(2)}, u32[]{:S(2)}) collective-permute-start(f32[4,16,128]{2,1,0:T(8,128)S(1)} %fusion.85), channel_id=1, source_target_pairs={{3,0},{4,1},{5,2},{6,3},{7,4},{11,8},{12,9},{13,10},{14,11},{15,12... | collective-permute-start | bytes 98312 | tf_op jit(solution)/shard_map/ppermute | solution.py:15
  211.5 12.4 %collective-permute-start.22 = (f32[4,16,128]{2,1,0:T(8,128)S(1)}, f32[4,16,128]{2,1,0:T(8,128)S(1)}, u32[]{:S(2)}, u32[]{:S(2)}) collective-permute-start(f32[4,16,128]{2,1,0:T(8,128)S(1)} %fusion.85), channel_id=1, source_target_pairs={{2,0},{3,1},{4,2},{5,3},{6,4},{7,5},{10,8},{11,9},{12,10},{13,11},... | collective-permute-start | bytes 98312 | tf_op jit(solution)/shard_map/ppermute | solution.py:15
  212.8 11.1 %collective-permute-start.21 = (f32[4,16,128]{2,1,0:T(8,128)S(1)}, f32[4,16,128]{2,1,0:T(8,128)S(1)}, u32[]{:S(2)}, u32[]{:S(2)}) collective-permute-start(f32[4,16,128]{2,1,0:T(8,128)S(1)} %fusion.85), channel_id=1, source_target_pairs={{1,0},{2,1},{3,2},{4,3},{5,4},{6,5},{7,6},{9,8},{10,9},{11,10},{12... | collective-permute-start | bytes 98312 | tf_op jit(solution)/shard_map/ppermute | solution.py:15
  214.7 9.1 %collective-permute-start.20 = (f32[4,16,128]{2,1,0:T(8,128)S(1)}, f32[4,16,128]{2,1,0:T(8,128)S(1)}, u32[]{:S(2)}, u32[]{:S(2)}) collective-permute-start(f32[4,16,128]{2,1,0:T(8,128)S(1)} %fusion.85), channel_id=1, source_target_pairs={{0,1},{1,2},{2,3},{3,4},{4,5},{5,6},{6,7},{8,9},{9,10},{10,11},{11... | collective-permute-start | bytes 98312 | tf_op jit(solution)/shard_map/ppermute | solution.py:15
  218.8 5.0 %collective-permute-start.19 = (f32[4,16,128]{2,1,0:T(8,128)S(1)}, f32[4,16,128]{2,1,0:T(8,128)S(1)}, u32[]{:S(2)}, u32[]{:S(2)}) collective-permute-start(f32[4,16,128]{2,1,0:T(8,128)S(1)} %fusion.85), channel_id=1, source_target_pairs={{0,2},{1,3},{2,4},{3,5},{4,6},{5,7},{8,10},{9,11},{10,12},{11,13},... | collective-permute-start | bytes 98312 | tf_op jit(solution)/shard_map/ppermute | solution.py:15
  286.6 10.9 %collective-permute-start.24 = (f32[4,16,128]{2,1,0:T(8,128)S(1)}, f32[4,16,128]{2,1,0:T(8,128)S(1)}, u32[]{:S(2)}, u32[]{:S(2)}) collective-permute-start(f32[4,16,128]{2,1,0:T(8,128)S(1)} %fusion.3), channel_id=1, source_target_pairs={{0,3},{1,4},{2,5},{3,6},{4,7},{8,11},{9,12},{10,13},{11,14},{12,15... | collective-permute-start | bytes 98312 | tf_op jit(solution)/shard_map/ppermute | solution.py:15
  288.1 14.6 %collective-permute-start.29 = (f32[4,16,128]{2,1,0:T(8,128)S(1)}, f32[4,16,128]{2,1,0:T(8,128)S(1)}, u32[]{:S(2)}, u32[]{:S(2)}) collective-permute-start(f32[4,16,128]{2,1,0:T(8,128)S(1)} %fusion.3), channel_id=1, source_target_pairs={{3,0},{4,1},{5,2},{6,3},{7,4},{11,8},{12,9},{13,10},{14,11},{15,12... | collective-permute-start | bytes 98312 | tf_op jit(solution)/shard_map/ppermute | solution.py:15
  289.4 13.2 %collective-permute-start.28 = (f32[4,16,128]{2,1,0:T(8,128)S(1)}, f32[4,16,128]{2,1,0:T(8,128)S(1)}, u32[]{:S(2)}, u32[]{:S(2)}) collective-permute-start(f32[4,16,128]{2,1,0:T(8,128)S(1)} %fusion.3), channel_id=1, source_target_pairs={{2,0},{3,1},{4,2},{5,3},{6,4},{7,5},{10,8},{11,9},{12,10},{13,11},... | collective-permute-start | bytes 98312 | tf_op jit(solution)/shard_map/ppermute | solution.py:15
  290.7 11.9 %collective-permute-start.27 = (f32[4,16,128]{2,1,0:T(8,128)S(1)}, f32[4,16,128]{2,1,0:T(8,128)S(1)}, u32[]{:S(2)}, u32[]{:S(2)}) collective-permute-start(f32[4,16,128]{2,1,0:T(8,128)S(1)} %fusion.3), channel_id=1, source_target_pairs={{1,0},{2,1},{3,2},{4,3},{5,4},{6,5},{7,6},{9,8},{10,9},{11,10},{12... | collective-permute-start | bytes 98312 | tf_op jit(solution)/shard_map/ppermute | solution.py:15
  293.4 9.2 %collective-permute-start.26 = (f32[4,16,128]{2,1,0:T(8,128)S(1)}, f32[4,16,128]{2,1,0:T(8,128)S(1)}, u32[]{:S(2)}, u32[]{:S(2)}) collective-permute-start(f32[4,16,128]{2,1,0:T(8,128)S(1)} %fusion.3), channel_id=1, source_target_pairs={{0,1},{1,2},{2,3},{3,4},{4,5},{5,6},{6,7},{8,9},{9,10},{10,11},{11... | collective-permute-start | bytes 98312 | tf_op jit(solution)/shard_map/ppermute | solution.py:15
  297.5 5.0 %collective-permute-start.25 = (f32[4,16,128]{2,1,0:T(8,128)S(1)}, f32[4,16,128]{2,1,0:T(8,128)S(1)}, u32[]{:S(2)}, u32[]{:S(2)}) collective-permute-start(f32[4,16,128]{2,1,0:T(8,128)S(1)} %fusion.3), channel_id=1, source_target_pairs={{0,2},{1,3},{2,4},{3,5},{4,6},{5,7},{8,10},{9,11},{10,12},{11,13},... | collective-permute-start | bytes 98312 | tf_op jit(solution)/shard_map/ppermute | solution.py:15
  331.7 38.4 %copy-start.2 = (f32[4,16,128]{2,1,0:T(8,128)}, f32[4,16,128]{2,1,0:T(8,128)S(1)}, u32[]{:S(2)}) copy-start(f32[4,16,128]{2,1,0:T(8,128)S(1)} %fusion.2) | copy-start | bytes 98308
  331.7 18.6 %collective-permute-start.30 = (f32[4,16,128]{2,1,0:T(8,128)S(1)}, f32[4,16,128]{2,1,0:T(8,128)S(1)}, u32[]{:S(2)}, u32[]{:S(2)}) collective-permute-start(f32[4,16,128]{2,1,0:T(8,128)S(1)} %fusion.2), channel_id=1, source_target_pairs={{0,3},{1,4},{2,5},{3,6},{4,7},{5,8},{6,9},{7,10},{8,11},{9,12},{10... | collective-permute-start | bytes 98312 | tf_op jit(solution)/shard_map/ppermute | solution.py:15
  333.6 25.7 %collective-permute-start.35 = (f32[4,16,128]{2,1,0:T(8,128)S(1)}, f32[4,16,128]{2,1,0:T(8,128)S(1)}, u32[]{:S(2)}, u32[]{:S(2)}) collective-permute-start(f32[4,16,128]{2,1,0:T(8,128)S(1)} %fusion.2), channel_id=1, source_target_pairs={{3,0},{4,1},{5,2},{6,3},{7,4},{8,5},{9,6},{10,7},{11,8},{12,9},{13... | collective-permute-start | bytes 98312 | tf_op jit(solution)/shard_map/ppermute | solution.py:15
  340.9 18.4 %collective-permute-start.34 = (f32[4,16,128]{2,1,0:T(8,128)S(1)}, f32[4,16,128]{2,1,0:T(8,128)S(1)}, u32[]{:S(2)}, u32[]{:S(2)}) collective-permute-start(f32[4,16,128]{2,1,0:T(8,128)S(1)} %fusion.2), channel_id=1, source_target_pairs={{2,0},{3,1},{4,2},{5,3},{6,4},{7,5},{8,6},{9,7},{10,8},{11,9},{12,... | collective-permute-start | bytes 98312 | tf_op jit(solution)/shard_map/ppermute | solution.py:15
  342.8 16.4 %collective-permute-start.33 = (f32[4,16,128]{2,1,0:T(8,128)S(1)}, f32[4,16,128]{2,1,0:T(8,128)S(1)}, u32[]{:S(2)}, u32[]{:S(2)}) collective-permute-start(f32[4,16,128]{2,1,0:T(8,128)S(1)} %fusion.2), channel_id=1, source_target_pairs={{1,0},{2,1},{3,2},{4,3},{5,4},{6,5},{7,6},{8,7},{9,8},{10,9},{11,1... | collective-permute-start | bytes 98312 | tf_op jit(solution)/shard_map/ppermute | solution.py:15
  346.8 12.4 %collective-permute-start.32 = (f32[4,16,128]{2,1,0:T(8,128)S(1)}, f32[4,16,128]{2,1,0:T(8,128)S(1)}, u32[]{:S(2)}, u32[]{:S(2)}) collective-permute-start(f32[4,16,128]{2,1,0:T(8,128)S(1)} %fusion.2), channel_id=1, source_target_pairs={{0,1},{1,2},{2,3},{3,4},{4,5},{5,6},{6,7},{7,8},{8,9},{9,10},{10,1... | collective-permute-start | bytes 98312 | tf_op jit(solution)/shard_map/ppermute | solution.py:15
  350.3 8.9 %collective-permute-start.31 = (f32[4,16,128]{2,1,0:T(8,128)S(1)}, f32[4,16,128]{2,1,0:T(8,128)S(1)}, u32[]{:S(2)}, u32[]{:S(2)}) collective-permute-start(f32[4,16,128]{2,1,0:T(8,128)S(1)} %fusion.2), channel_id=1, source_target_pairs={{0,2},{1,3},{2,4},{3,5},{4,6},{5,7},{6,8},{7,9},{8,10},{9,11},{10,... | collective-permute-start | bytes 98312 | tf_op jit(solution)/shard_map/ppermute | solution.py:15
where the time goes:
time: 372 us; the launch traced here: 370 us
  blocking collectives  128 us (34%)
  starting transfers between devices  113 us (30%)
  matrix products  64.6 us (17%)
  waiting for transfers between devices  30.9 us (8%)
  other arithmetic  24.9 us (7%)
  local copies, waits for them, and re-layouts  6.56 us (2%)
    ppermute x36, starting transfers between devices, from_behind(): lax.ppermute(value, axis, [(source, source + steps) for source in range(f...  113 us
    dot_general x6, matrix products, tile_product(): jnp.einsum('ikab,ikcb->ica', matrix_tiles, picked, precision=lax.Precisio...  57 us
    psum x1, blocking collectives, per_device(): lax.psum((inner_products(direction, applied), inner_products(applied, res...  36.1 us
    psum x1, blocking collectives, per_device(): squares = lax.psum(inner_products(residual, residual), ('grp', 'row'))  36.1 us
    ppermute x36, waiting for transfers between devices, from_behind(): lax.ppermute(value, axis, [(source, source + steps) for source in range(f...  30.9 us
    psum x1, blocking collectives, per_device(): weight = lax.psum(inner_products(remainder, smoothed), 'row')  24.9 us
    psum x1, blocking collectives, per_device(): weight_next = lax.psum(inner_products(remainder, smoothed), 'row')  17.3 us
    psum x1, blocking collectives, per_device(): bending = lax.psum(inner_products(heading, applied), 'row')  13.9 us
  transfers between devices with their start and end apart: 36, of which 7 were waited for; matrix products, arithmetic and copies ran while one was open for 1% of the time, Pallas kernels for 0%

commit v1 on v0

--- a/solution.py
+++ b/solution.py
@@ -74,7 +74,7 @@
     solution = jnp.zeros_like(right_side)
     residual = right_side
     direction = right_side
-    squares = lax.psum(inner_products(residual, residual), ("grp", "row"))
+    squares = lax.psum(lax.psum(inner_products(residual, residual), "row"), "grp")
     for outer_step in range(OUTER):
         applied = full_product(direction)
         curvature, crossed, square = lax.psum(

time: 372 us -> 393 us (1.056)
  blocking collectives: 128 us -> 155 us
  waiting for transfers between devices: 30.9 us -> 26.5 us
    psum x1 -> x2, blocking collectives: 36.1 us -> 78.2 us  [per_device(): lax.psum((inner_products(direction, applied), inner_products(applied, res...]
    psum x1 -> x2, blocking collectives: 36.1 us -> 20.9 us  [the longest x1 13.8 us: per_device(): lax.psum(inner_products(residual, residual), 'row')]
    ppermute x36, waiting for transfers between devices: 30.9 us -> 26.5 us  [from_behind(): lax.ppermute(value, axis, [(source, source + steps) for source in range(f...]
  transfers between devices with their start and end apart: 36 -> 36, of which waited for: 7 -> 6; matrix products, arithmetic and copies ran while one was open for 1% -> 2% of each run, Pallas kernels for 0% -> 0%
where the time goes in v1:
time: 393 us; the launch traced here: 392 us
  blocking collectives  155 us (39%)
  starting transfers between devices  112 us (28%)
  matrix products  64.6 us (16%)
  waiting for transfers between devices  26.5 us (7%)
  other arithmetic  24.9 us (6%)
  local copies, waits for them, and re-layouts  6.56 us (2%)
    ppermute x36, starting transfers between devices, from_behind(): lax.ppermute(value, axis, [(source, source + steps) for source in range(f...  112 us
    psum x2, blocking collectives, per_device(): lax.psum((inner_products(direction, applied), inner_products(applied, res...  78.2 us
    dot_general x6, matrix products, tile_product(): jnp.einsum('ikab,ikcb->ica', matrix_tiles, picked, precision=lax.Precisio...  57 us
    ppermute x36, waiting for transfers between devices, from_behind(): lax.ppermute(value, axis, [(source, source + steps) for source in range(f...  26.5 us
    psum x1, blocking collectives, per_device(): weight = lax.psum(inner_products(remainder, smoothed), 'row')  24.9 us
    psum x1, blocking collectives, per_device(): weight_next = lax.psum(inner_products(remainder, smoothed), 'row')  17.3 us
    psum x1, blocking collectives, per_device(): bending = lax.psum(inner_products(heading, applied), 'row')  13.9 us
    psum x1, blocking collectives, per_device(): lax.psum(inner_products(residual, residual), 'row')  13.8 us
  transfers between devices with their start and end apart: 36, of which 6 were waited for; matrix products, arithmetic and copies ran while one was open for 2% of the time, Pallas kernels for 0%

profile of v1, /device:TPU:5, one launch (start us, length us, event | category | flops | bytes accessed | tf_op | source)
XLA Modules:
  0.0 391.6 jit_solution(1725631330179012455)
XLA Ops:
  0.6 6.8 %collective-permute-start.5 = (f32[4,16,128]{2,1,0:T(8,128)}, f32[4,16,128]{2,1,0:T(8,128)S(1)}, u32[]{:S(2)}, u32[]{:S(2)}) collective-permute-start(f32[4,16,128]{2,1,0:T(8,128)} %param.15), channel_id=1, source_target_pairs={{3,0},{4,1},{5,2},{6,3},{7,4},{8,5},{9,6},{10,7},{11,8},{12,9},{13... | collective-permute-start | bytes 98312 | tf_op jit(solution)/shard_map/ppermute | solution.py:15
  7.4 2.1 collective-permute-start.4
  9.5 2.1 collective-permute-start.3
  11.7 3.4 collective-permute-start.2
  15.1 2.9 collective-permute-start
  19.8 13.8 %psum.71 = f32[16,16]{1,0:T(8,128)S(1)} all-reduce(f32[16,16]{1,0:T(8,128)S(1)} %convolution_bitcast_fusion.21), channel_id=1, replica_groups=mesh['grp'=4,'row'=8] {'row'}, use_global_device_ids=true, to_apply=%region_3.6 | all-reduce | flops 256 | bytes 2048 | tf_op jit(solution)/shard_map/psum | solution.py:77
  33.6 7.1 %psum.72 = f32[16,16]{1,0:T(8,128)S(1)} all-reduce(f32[16,16]{1,0:T(8,128)S(1)} %psum.71), channel_id=1, replica_groups=mesh['grp'=4,'row'=8] {'grp'}, use_global_device_ids=true, to_apply=%region_4.7 | all-reduce | flops 256 | bytes 2048 | tf_op jit(solution)/shard_map/psum | solution.py:77
  40.9 1.5 cholesky.115
  43.7 1.2 custom-call.21
  44.9 1.9 collective-permute-start.1
  46.9 6.5 %collective-permute-done.1 = f32[4,16,128]{2,1,0:T(8,128)S(1)} collective-permute-done((f32[4,16,128]{2,1,0:T(8,128)}, f32[4,16,128]{2,1,0:T(8,128)S(1)}, u32[]{:S(2)}, u32[]{:S(2)}) %collective-permute-start.1) | collective-permute-done | bytes 32800 | tf_op jit(solution)/shard_map/ppermute | solution.py:15
  55.0 9.4 %convolution_bitcast_fusion.9 = f32[4,16,128]{2,1,0:T(8,128)S(1)} fusion(f32[4,32,128,128]{3,2,1,0:T(8,128)} %param.12, f32[4,32,16,128]{3,2,1,0:T(8,128)S(1)} %bitcast.254, pred[4,32]{1,0:T(4,128)(4,1)S(1)} %get-tuple-element.13), kind=kOutput, calls=%fused_computation.26 | convolution fusion | flops 402915328 | bytes 9470080 | tf_op jit(solution)/shard_map/ikab,ikcb->ica/dot_general | solution.py:56
  64.8 42.0 %all-reduce = (f32[16,16]{1,0:T(8,128)S(1)}, f32[16,16]{1,0:T(8,128)S(1)}, f32[16,16]{1,0:T(8,128)S(1)}) all-reduce(f32[16,16]{1,0:T(8,128)S(1)} %bitcast.256, f32[16,16]{1,0:T(8,128)S(1)} %convolution_bitcast_fusion.22, f32[16,16]{1,0:T(8,128)S(1)} %convolution_bitcast_fusion.20), channel_id=1, replica_groups=mesh['grp'=4,'row'=8] {'grp','row'}, use_global_device_ids=true, to_apply=%region_0.2 | all-reduce | flops 768 | bytes 6144 | tf_op jit(solution)/shard_map/psum | solution.py:80
  107.0 1.5 cholesky.104
  109.8 1.2 custom-call.19
  112.9 5.4 %collective-permute-start.6 = (f32[4,16,128]{2,1,0:T(8,128)S(1)}, f32[4,16,128]{2,1,0:T(8,128)S(1)}, u32[]{:S(2)}, u32[]{:S(2)}) collective-permute-start(f32[4,16,128]{2,1,0:T(8,128)S(1)} %fusion.7), channel_id=1, source_target_pairs={{0,3},{1,4},{2,5},{3,6},{4,7},{5,8},{6,9},{7,10},{8,11},{9,12},{10... | collective-permute-start | bytes 98312 | tf_op jit(solution)/shard_map/ppermute | solution.py:15
  118.6 3.7 collective-permute-start.11
  122.3 3.8 collective-permute-start.10
  126.2 1.9 collective-permute-start.9
  128.1 3.6 collective-permute-start.8
  131.7 2.5 collective-permute-start.7
  134.2 5.8 %collective-permute-done.7 = f32[4,16,128]{2,1,0:T(8,128)S(1)} collective-permute-done((f32[4,16,128]{2,1,0:T(8,128)S(1)}, f32[4,16,128]{2,1,0:T(8,128)S(1)}, u32[]{:S(2)}, u32[]{:S(2)}) %collective-permute-start.7) | collective-permute-done | bytes 32800 | tf_op jit(solution)/shard_map/ppermute | solution.py:15
  140.9 9.4 %convolution_bitcast_fusion.6 = f32[4,16,128]{2,1,0:T(8,128)S(1)} fusion(f32[4,32,128,128]{3,2,1,0:T(8,128)} %param.12, f32[4,32,16,128]{3,2,1,0:T(8,128)S(1)} %bitcast.255, pred[4,32]{1,0:T(4,128)(4,1)S(1)} %get-tuple-element.13), kind=kOutput, calls=%fused_computation.21 | convolution fusion | flops 402915328 | bytes 9470080 | tf_op jit(solution)/shard_map/ikab,ikcb->ica/dot_general | solution.py:56
  150.4 36.1 %psum.75 = f32[16,16]{1,0:T(8,128)S(1)} all-reduce(f32[16,16]{1,0:T(8,128)S(1)} %convolution_bitcast_fusion.18), channel_id=1, replica_groups=mesh['grp'=4,'row'=8] {'grp','row'}, use_global_device_ids=true, to_apply=%region_7.12 | all-reduce | flops 256 | bytes 2048 | tf_op jit(solution)/shard_map/psum | solution.py:80
  186.7 1.5 cholesky.126
  189.5 1.2 custom-call.23
  191.3 6.0 %collective-permute-start.12 = (f32[4,16,128]{2,1,0:T(8,128)S(1)}, f32[4,16,128]{2,1,0:T(8,128)S(1)}, u32[]{:S(2)}, u32[]{:S(2)}) collective-permute-start(f32[4,16,128]{2,1,0:T(8,128)S(1)} %fusion.6), channel_id=1, source_target_pairs={{0,3},{1,4},{2,5},{3,6},{4,7},{5,8},{6,9},{7,10},{8,11},{9,12},{10... | collective-permute-start | bytes 98312 | tf_op jit(solution)/shard_map/ppermute | solution.py:15
  198.0 3.2 collective-permute-start.17
  201.2 4.4 %collective-permute-start.16 = (f32[4,16,128]{2,1,0:T(8,128)S(1)}, f32[4,16,128]{2,1,0:T(8,128)S(1)}, u32[]{:S(2)}, u32[]{:S(2)}) collective-permute-start(f32[4,16,128]{2,1,0:T(8,128)S(1)} %fusion.6), channel_id=1, source_target_pairs={{2,0},{3,1},{4,2},{5,3},{6,4},{7,5},{8,6},{9,7},{10,8},{11,9},{12,... | collective-permute-start | bytes 98312 | tf_op jit(solution)/shard_map/ppermute | solution.py:15
  205.6 1.9 collective-permute-start.15
  207.6 3.6 collective-permute-start.14
  211.2 2.7 collective-permute-start.13
  213.9 5.6 %collective-permute-done.13 = f32[4,16,128]{2,1,0:T(8,128)S(1)} collective-permute-done((f32[4,16,128]{2,1,0:T(8,128)S(1)}, f32[4,16,128]{2,1,0:T(8,128)S(1)}, u32[]{:S(2)}, u32[]{:S(2)}) %collective-permute-start.13) | collective-permute-done | bytes 32800 | tf_op jit(solution)/shard_map/ppermute | solution.py:15
  220.3 9.4 %fusion.5 = f32[4,16,128]{2,1,0:T(8,128)S(1)} fusion(f32[4,16,128]{2,1,0:T(8,128)S(1)} %copy-done.1, f32[4,32,128,128]{3,2,1,0:T(8,128)} %param.12, f32[4,32,16,128]{3,2,1,0:T(8,128)S(1)} %bitcast.250, f32[4,32]{1,0:T(4,128)S(1)} %get-tuple-element.12, pred[4,32]{1,0:T(4,128)(4,1)S(1)} %get-tuple-element.13), kind=kOutput, calls=%fused_computation.18 | convolution fusion | flops 403185664 | bytes 9503360 | tf_op jit(solution)/shard_map/ikab,ikcb->ica/dot_general | solution.py:56
  230.3 1.3 collective-permute-start.18
  231.7 1.3 collective-permute-start.23
  233.0 1.3 collective-permute-start.22
  234.3 1.9 collective-permute-start.21
  236.3 4.1 %collective-permute-start.20 = (f32[4,16,128]{2,1,0:T(8,128)S(1)}, f32[4,16,128]{2,1,0:T(8,128)S(1)}, u32[]{:S(2)}, u32[]{:S(2)}) collective-permute-start(f32[4,16,128]{2,1,0:T(8,128)S(1)} %fusion.85), channel_id=1, source_target_pairs={{0,1},{1,2},{2,3},{3,4},{4,5},{5,6},{6,7},{8,9},{9,10},{10,11},{11... | collective-permute-start | bytes 98312 | tf_op jit(solution)/shard_map/ppermute | solution.py:15
  240.4 4.0 %collective-permute-start.19 = (f32[4,16,128]{2,1,0:T(8,128)S(1)}, f32[4,16,128]{2,1,0:T(8,128)S(1)}, u32[]{:S(2)}, u32[]{:S(2)}) collective-permute-start(f32[4,16,128]{2,1,0:T(8,128)S(1)} %fusion.85), channel_id=1, source_target_pairs={{0,2},{1,3},{2,4},{3,5},{4,6},{5,7},{8,10},{9,11},{10,12},{11,13},... | collective-permute-start | bytes 98312 | tf_op jit(solution)/shard_map/ppermute | solution.py:15
  246.2 9.4 %convolution_bitcast_fusion.4 = f32[4,16,128]{2,1,0:T(8,128)S(1)} fusion(f32[4,32,128,128]{3,2,1,0:T(8,128)} %param.12, f32[4,32,16,128]{3,2,1,0:T(8,128)S(1)} %bitcast.251, f32[4,32]{1,0:T(4,128)S(1)} %get-tuple-element.11, pred[4,32]{1,0:T(4,128)(4,1)S(1)} %get-tuple-element.13), kind=kOutput, calls=%fused_computation.16 | convolution fusion | flops 403177472 | bytes 9470592 | tf_op jit(solution)/shard_map/ikab,ikcb->ica/dot_general | solution.py:56
  255.8 24.9 %all-reduce.1 = (f32[16,16]{1,0:T(8,128)S(1)}, f32[16,16]{1,0:T(8,128)S(1)}) all-reduce(f32[16,16]{1,0:T(8,128)S(1)} %convolution_bitcast_fusion.15, f32[16,16]{1,0:T(8,128)S(1)} %convolution_bitcast_fusion.16), channel_id=1, replica_groups=mesh['grp'=4,'row'=8] {'row'}, use_global_device_ids=true, to_apply=%region_9.14 | all-reduce | flops 512 | bytes 4096 | tf_op jit(solution)/shard_map/psum | solution.py:110
  280.9 1.5 cholesky.148
  283.7 1.2 custom-call.27
  285.0 1.5 cholesky.137
  287.8 1.2 custom-call.25
  290.3 17.3 %psum.78 = f32[16,16]{1,0:T(8,128)S(1)} all-reduce(f32[16,16]{1,0:T(8,128)S(1)} %convolution_bitcast_fusion.13), channel_id=1, replica_groups=mesh['grp'=4,'row'=8] {'row'}, use_global_device_ids=true, to_apply=%region_10.15 | all-reduce | flops 256 | bytes 2048 | tf_op jit(solution)/shard_map/psum | solution.py:121
  308.2 1.3 collective-permute-start.24
  309.6 1.3 collective-permute-start.29
  310.9 1.3 collective-permute-start.28
  312.2 2.7 collective-permute-start.27
  314.9 4.2 %collective-permute-start.26 = (f32[4,16,128]{2,1,0:T(8,128)S(1)}, f32[4,16,128]{2,1,0:T(8,128)S(1)}, u32[]{:S(2)}, u32[]{:S(2)}) collective-permute-start(f32[4,16,128]{2,1,0:T(8,128)S(1)} %fusion.3), channel_id=1, source_target_pairs={{0,1},{1,2},{2,3},{3,4},{4,5},{5,6},{6,7},{8,9},{9,10},{10,11},{11... | collective-permute-start | bytes 98312 | tf_op jit(solution)/shard_map/ppermute | solution.py:15
  319.1 4.2 %collective-permute-start.25 = (f32[4,16,128]{2,1,0:T(8,128)S(1)}, f32[4,16,128]{2,1,0:T(8,128)S(1)}, u32[]{:S(2)}, u32[]{:S(2)}) collective-permute-start(f32[4,16,128]{2,1,0:T(8,128)S(1)} %fusion.3), channel_id=1, source_target_pairs={{0,2},{1,3},{2,4},{3,5},{4,6},{5,7},{8,10},{9,11},{10,12},{11,13},... | collective-permute-start | bytes 98312 | tf_op jit(solution)/shard_map/ppermute | solution.py:15
  325.0 9.4 %convolution_bitcast_fusion.1 = f32[4,16,128]{2,1,0:T(8,128)S(1)} fusion(f32[4,32,128,128]{3,2,1,0:T(8,128)} %param.12, f32[4,32,16,128]{3,2,1,0:T(8,128)S(1)} %bitcast.252, f32[4,32]{1,0:T(4,128)S(1)} %get-tuple-element.11, pred[4,32]{1,0:T(4,128)(4,1)S(1)} %get-tuple-element.13), kind=kOutput, calls=%fused_computation.11 | convolution fusion | flops 403177472 | bytes 9470592 | tf_op jit(solution)/shard_map/ikab,ikcb->ica/dot_general | solution.py:56
  334.5 13.9 %psum.79 = f32[16,16]{1,0:T(8,128)S(1)} all-reduce(f32[16,16]{1,0:T(8,128)S(1)} %convolution_bitcast_fusion.11), channel_id=1, replica_groups=mesh['grp'=4,'row'=8] {'row'}, use_global_device_ids=true, to_apply=%region_11.16 | all-reduce | flops 256 | bytes 2048 | tf_op jit(solution)/shard_map/psum | solution.py:115
  348.6 1.5 cholesky.159
  353.3 1.9 collective-permute-start.30
  355.2 7.2 %collective-permute-start.35 = (f32[4,16,128]{2,1,0:T(8,128)S(1)}, f32[4,16,128]{2,1,0:T(8,128)S(1)}, u32[]{:S(2)}, u32[]{:S(2)}) collective-permute-start(f32[4,16,128]{2,1,0:T(8,128)S(1)} %fusion.2), channel_id=1, source_target_pairs={{3,0},{4,1},{5,2},{6,3},{7,4},{8,5},{9,6},{10,7},{11,8},{12,9},{13... | collective-permute-start | bytes 98312 | tf_op jit(solution)/shard_map/ppermute | solution.py:15
  362.4 1.9 collective-permute-start.34
  364.4 4.0 %collective-permute-start.33 = (f32[4,16,128]{2,1,0:T(8,128)S(1)}, f32[4,16,128]{2,1,0:T(8,128)S(1)}, u32[]{:S(2)}, u32[]{:S(2)}) collective-permute-start(f32[4,16,128]{2,1,0:T(8,128)S(1)} %fusion.2), channel_id=1, source_target_pairs={{1,0},{2,1},{3,2},{4,3},{5,4},{6,5},{7,6},{8,7},{9,8},{10,9},{11,1... | collective-permute-start | bytes 98312 | tf_op jit(solution)/shard_map/ppermute | solution.py:15
  368.3 3.5 collective-permute-start.32
  371.9 2.0 collective-permute-start.31
  373.9 6.8 %collective-permute-done.31 = f32[4,16,128]{2,1,0:T(8,128)S(1)} collective-permute-done((f32[4,16,128]{2,1,0:T(8,128)S(1)}, f32[4,16,128]{2,1,0:T(8,128)S(1)}, u32[]{:S(2)}, u32[]{:S(2)}) %collective-permute-start.31) | collective-permute-done | bytes 32800 | tf_op jit(solution)/shard_map/ppermute | solution.py:15
  381.6 10.0 %fusion = f32[4,16,128]{2,1,0:T(8,128)} fusion(f32[4,16,128]{2,1,0:T(8,128)S(1)} %copy-done.1, f32[4,32,128,128]{3,2,1,0:T(8,128)} %param.12, f32[4,32,16,128]{3,2,1,0:T(8,128)S(1)} %bitcast.253, pred[4,32]{1,0:T(4,128)(4,1)S(1)} %get-tuple-element.13), kind=kOutput, calls=%fused_computation.7 | convolution fusion | flops 402923520 | bytes 9502848 | tf_op jit(solution)/shard_map/ikab,ikcb->ica/dot_general | solution.py:56
  (169 shorter events, 26.0 us)
Async XLA Ops:
  0.6 229.1 %copy-start = (f32[4,128,128]{2,1,0:T(8,128)S(1)}, f32[4,128,128]{2,1,0:T(8,128)}, u32[]{:S(2)}) copy-start(f32[4,128,128]{2,1,0:T(8,128)} %param.14) | copy-start | bytes 786436
  0.6 53.6 %collective-permute-start.5 = (f32[4,16,128]{2,1,0:T(8,128)}, f32[4,16,128]{2,1,0:T(8,128)S(1)}, u32[]{:S(2)}, u32[]{:S(2)}) collective-permute-start(f32[4,16,128]{2,1,0:T(8,128)} %param.15), channel_id=1, source_target_pairs={{3,0},{4,1},{5,2},{6,3},{7,4},{8,5},{9,6},{10,7},{11,8},{12,9},{13... | collective-permute-start | bytes 98312 | tf_op jit(solution)/shard_map/ppermute | solution.py:15
  7.4 46.7 %collective-permute-start.4 = (f32[4,16,128]{2,1,0:T(8,128)}, f32[4,16,128]{2,1,0:T(8,128)S(1)}, u32[]{:S(2)}, u32[]{:S(2)}) collective-permute-start(f32[4,16,128]{2,1,0:T(8,128)} %param.15), channel_id=1, source_target_pairs={{2,0},{3,1},{4,2},{5,3},{6,4},{7,5},{8,6},{9,7},{10,8},{11,9},{12,... | collective-permute-start | bytes 98312 | tf_op jit(solution)/shard_map/ppermute | solution.py:15
  9.5 44.6 %collective-permute-start.3 = (f32[4,16,128]{2,1,0:T(8,128)}, f32[4,16,128]{2,1,0:T(8,128)S(1)}, u32[]{:S(2)}, u32[]{:S(2)}) collective-permute-start(f32[4,16,128]{2,1,0:T(8,128)} %param.15), channel_id=1, source_target_pairs={{1,0},{2,1},{3,2},{4,3},{5,4},{6,5},{7,6},{8,7},{9,8},{10,9},{11,1... | collective-permute-start | bytes 98312 | tf_op jit(solution)/shard_map/ppermute | solution.py:15
  11.7 41.7 %collective-permute-start.2 = (f32[4,16,128]{2,1,0:T(8,128)}, f32[4,16,128]{2,1,0:T(8,128)S(1)}, u32[]{:S(2)}, u32[]{:S(2)}) collective-permute-start(f32[4,16,128]{2,1,0:T(8,128)} %param.15), channel_id=1, source_target_pairs={{0,1},{1,2},{2,3},{3,4},{4,5},{5,6},{6,7},{7,8},{8,9},{9,10},{10,1... | collective-permute-start | bytes 98312 | tf_op jit(solution)/shard_map/ppermute | solution.py:15
  15.1 29.8 %collective-permute-start = (f32[4,16,128]{2,1,0:T(8,128)}, f32[4,16,128]{2,1,0:T(8,128)S(1)}, u32[]{:S(2)}, u32[]{:S(2)}) collective-permute-start(f32[4,16,128]{2,1,0:T(8,128)} %param.15), channel_id=1, source_target_pairs={{0,3},{1,4},{2,5},{3,6},{4,7},{5,8},{6,9},{7,10},{8,11},{9,12},{10... | collective-permute-start | bytes 98312 | tf_op jit(solution)/shard_map/ppermute | solution.py:15
  42.4 22.0 %copy-start.1 = (f32[4,16,128]{2,1,0:T(8,128)S(1)}, f32[4,16,128]{2,1,0:T(8,128)}, u32[]{:S(2)}) copy-start(f32[4,16,128]{2,1,0:T(8,128)} %param.15) | copy-start | bytes 98308
  44.9 8.5 %collective-permute-start.1 = (f32[4,16,128]{2,1,0:T(8,128)}, f32[4,16,128]{2,1,0:T(8,128)S(1)}, u32[]{:S(2)}, u32[]{:S(2)}) collective-permute-start(f32[4,16,128]{2,1,0:T(8,128)} %param.15), channel_id=1, source_target_pairs={{0,2},{1,3},{2,4},{3,5},{4,6},{5,7},{6,8},{7,9},{8,10},{9,11},{10,... | collective-permute-start | bytes 98312 | tf_op jit(solution)/shard_map/ppermute | solution.py:15
  112.9 18.8 %collective-permute-start.6 = (f32[4,16,128]{2,1,0:T(8,128)S(1)}, f32[4,16,128]{2,1,0:T(8,128)S(1)}, u32[]{:S(2)}, u32[]{:S(2)}) collective-permute-start(f32[4,16,128]{2,1,0:T(8,128)S(1)} %fusion.7), channel_id=1, source_target_pairs={{0,3},{1,4},{2,5},{3,6},{4,7},{5,8},{6,9},{7,10},{8,11},{9,12},{10... | collective-permute-start | bytes 98312 | tf_op jit(solution)/shard_map/ppermute | solution.py:15
  118.6 21.5 %collective-permute-start.11 = (f32[4,16,128]{2,1,0:T(8,128)S(1)}, f32[4,16,128]{2,1,0:T(8,128)S(1)}, u32[]{:S(2)}, u32[]{:S(2)}) collective-permute-start(f32[4,16,128]{2,1,0:T(8,128)S(1)} %fusion.7), channel_id=1, source_target_pairs={{3,0},{4,1},{5,2},{6,3},{7,4},{8,5},{9,6},{10,7},{11,8},{12,9},{13... | collective-permute-start | bytes 98312 | tf_op jit(solution)/shard_map/ppermute | solution.py:15
  122.3 17.7 %collective-permute-start.10 = (f32[4,16,128]{2,1,0:T(8,128)S(1)}, f32[4,16,128]{2,1,0:T(8,128)S(1)}, u32[]{:S(2)}, u32[]{:S(2)}) collective-permute-start(f32[4,16,128]{2,1,0:T(8,128)S(1)} %fusion.7), channel_id=1, source_target_pairs={{2,0},{3,1},{4,2},{5,3},{6,4},{7,5},{8,6},{9,7},{10,8},{11,9},{12,... | collective-permute-start | bytes 98312 | tf_op jit(solution)/shard_map/ppermute | solution.py:15
  126.2 13.9 %collective-permute-start.9 = (f32[4,16,128]{2,1,0:T(8,128)S(1)}, f32[4,16,128]{2,1,0:T(8,128)S(1)}, u32[]{:S(2)}, u32[]{:S(2)}) collective-permute-start(f32[4,16,128]{2,1,0:T(8,128)S(1)} %fusion.7), channel_id=1, source_target_pairs={{1,0},{2,1},{3,2},{4,3},{5,4},{6,5},{7,6},{8,7},{9,8},{10,9},{11,1... | collective-permute-start | bytes 98312 | tf_op jit(solution)/shard_map/ppermute | solution.py:15
  128.1 11.9 %collective-permute-start.8 = (f32[4,16,128]{2,1,0:T(8,128)S(1)}, f32[4,16,128]{2,1,0:T(8,128)S(1)}, u32[]{:S(2)}, u32[]{:S(2)}) collective-permute-start(f32[4,16,128]{2,1,0:T(8,128)S(1)} %fusion.7), channel_id=1, source_target_pairs={{0,1},{1,2},{2,3},{3,4},{4,5},{5,6},{6,7},{7,8},{8,9},{9,10},{10,1... | collective-permute-start | bytes 98312 | tf_op jit(solution)/shard_map/ppermute | solution.py:15
  131.7 8.3 %collective-permute-start.7 = (f32[4,16,128]{2,1,0:T(8,128)S(1)}, f32[4,16,128]{2,1,0:T(8,128)S(1)}, u32[]{:S(2)}, u32[]{:S(2)}) collective-permute-start(f32[4,16,128]{2,1,0:T(8,128)S(1)} %fusion.7), channel_id=1, source_target_pairs={{0,2},{1,3},{2,4},{3,5},{4,6},{5,7},{6,8},{7,9},{8,10},{9,11},{10,... | collective-permute-start | bytes 98312 | tf_op jit(solution)/shard_map/ppermute | solution.py:15
  140.1 57.2 %copy-start.3 = (s32[4,32]{1,0:T(4,128)S(1)}, s32[4,32]{1,0:T(4,128)}, u32[]{:S(2)}) copy-start(s32[4,32]{1,0:T(4,128)} %param.13) | copy-start | bytes 1540
  191.3 19.9 %collective-permute-start.12 = (f32[4,16,128]{2,1,0:T(8,128)S(1)}, f32[4,16,128]{2,1,0:T(8,128)S(1)}, u32[]{:S(2)}, u32[]{:S(2)}) collective-permute-start(f32[4,16,128]{2,1,0:T(8,128)S(1)} %fusion.6), channel_id=1, source_target_pairs={{0,3},{1,4},{2,5},{3,6},{4,7},{5,8},{6,9},{7,10},{8,11},{9,12},{10... | collective-permute-start | bytes 98312 | tf_op jit(solution)/shard_map/ppermute | solution.py:15
  198.0 21.6 %collective-permute-start.17 = (f32[4,16,128]{2,1,0:T(8,128)S(1)}, f32[4,16,128]{2,1,0:T(8,128)S(1)}, u32[]{:S(2)}, u32[]{:S(2)}) collective-permute-start(f32[4,16,128]{2,1,0:T(8,128)S(1)} %fusion.6), channel_id=1, source_target_pairs={{3,0},{4,1},{5,2},{6,3},{7,4},{8,5},{9,6},{10,7},{11,8},{12,9},{13... | collective-permute-start | bytes 98312 | tf_op jit(solution)/shard_map/ppermute | solution.py:15
  201.2 18.4 %collective-permute-start.16 = (f32[4,16,128]{2,1,0:T(8,128)S(1)}, f32[4,16,128]{2,1,0:T(8,128)S(1)}, u32[]{:S(2)}, u32[]{:S(2)}) collective-permute-start(f32[4,16,128]{2,1,0:T(8,128)S(1)} %fusion.6), channel_id=1, source_target_pairs={{2,0},{3,1},{4,2},{5,3},{6,4},{7,5},{8,6},{9,7},{10,8},{11,9},{12,... | collective-permute-start | bytes 98312 | tf_op jit(solution)/shard_map/ppermute | solution.py:15
  205.6 13.9 %collective-permute-start.15 = (f32[4,16,128]{2,1,0:T(8,128)S(1)}, f32[4,16,128]{2,1,0:T(8,128)S(1)}, u32[]{:S(2)}, u32[]{:S(2)}) collective-permute-start(f32[4,16,128]{2,1,0:T(8,128)S(1)} %fusion.6), channel_id=1, source_target_pairs={{1,0},{2,1},{3,2},{4,3},{5,4},{6,5},{7,6},{8,7},{9,8},{10,9},{11,1... | collective-permute-start | bytes 98312 | tf_op jit(solution)/shard_map/ppermute | solution.py:15
  207.6 11.9 %collective-permute-start.14 = (f32[4,16,128]{2,1,0:T(8,128)S(1)}, f32[4,16,128]{2,1,0:T(8,128)S(1)}, u32[]{:S(2)}, u32[]{:S(2)}) collective-permute-start(f32[4,16,128]{2,1,0:T(8,128)S(1)} %fusion.6), channel_id=1, source_target_pairs={{0,1},{1,2},{2,3},{3,4},{4,5},{5,6},{6,7},{7,8},{8,9},{9,10},{10,1... | collective-permute-start | bytes 98312 | tf_op jit(solution)/shard_map/ppermute | solution.py:15
  211.2 8.3 %collective-permute-start.13 = (f32[4,16,128]{2,1,0:T(8,128)S(1)}, f32[4,16,128]{2,1,0:T(8,128)S(1)}, u32[]{:S(2)}, u32[]{:S(2)}) collective-permute-start(f32[4,16,128]{2,1,0:T(8,128)S(1)} %fusion.6), channel_id=1, source_target_pairs={{0,2},{1,3},{2,4},{3,5},{4,6},{5,7},{6,8},{7,9},{8,10},{9,11},{10,... | collective-permute-start | bytes 98312 | tf_op jit(solution)/shard_map/ppermute | solution.py:15
  230.3 10.1 %collective-permute-start.18 = (f32[4,16,128]{2,1,0:T(8,128)S(1)}, f32[4,16,128]{2,1,0:T(8,128)S(1)}, u32[]{:S(2)}, u32[]{:S(2)}) collective-permute-start(f32[4,16,128]{2,1,0:T(8,128)S(1)} %fusion.85), channel_id=1, source_target_pairs={{0,3},{1,4},{2,5},{3,6},{4,7},{8,11},{9,12},{10,13},{11,14},{12,15... | collective-permute-start | bytes 98312 | tf_op jit(solution)/shard_map/ppermute | solution.py:15
  231.7 13.7 %collective-permute-start.23 = (f32[4,16,128]{2,1,0:T(8,128)S(1)}, f32[4,16,128]{2,1,0:T(8,128)S(1)}, u32[]{:S(2)}, u32[]{:S(2)}) collective-permute-start(f32[4,16,128]{2,1,0:T(8,128)S(1)} %fusion.85), channel_id=1, source_target_pairs={{3,0},{4,1},{5,2},{6,3},{7,4},{11,8},{12,9},{13,10},{14,11},{15,12... | collective-permute-start | bytes 98312 | tf_op jit(solution)/shard_map/ppermute | solution.py:15
  233.0 12.4 %collective-permute-start.22 = (f32[4,16,128]{2,1,0:T(8,128)S(1)}, f32[4,16,128]{2,1,0:T(8,128)S(1)}, u32[]{:S(2)}, u32[]{:S(2)}) collective-permute-start(f32[4,16,128]{2,1,0:T(8,128)S(1)} %fusion.85), channel_id=1, source_target_pairs={{2,0},{3,1},{4,2},{5,3},{6,4},{7,5},{10,8},{11,9},{12,10},{13,11},... | collective-permute-start | bytes 98312 | tf_op jit(solution)/shard_map/ppermute | solution.py:15
  234.3 11.1 %collective-permute-start.21 = (f32[4,16,128]{2,1,0:T(8,128)S(1)}, f32[4,16,128]{2,1,0:T(8,128)S(1)}, u32[]{:S(2)}, u32[]{:S(2)}) collective-permute-start(f32[4,16,128]{2,1,0:T(8,128)S(1)} %fusion.85), channel_id=1, source_target_pairs={{1,0},{2,1},{3,2},{4,3},{5,4},{6,5},{7,6},{9,8},{10,9},{11,10},{12... | collective-permute-start | bytes 98312 | tf_op jit(solution)/shard_map/ppermute | solution.py:15
  236.3 9.1 %collective-permute-start.20 = (f32[4,16,128]{2,1,0:T(8,128)S(1)}, f32[4,16,128]{2,1,0:T(8,128)S(1)}, u32[]{:S(2)}, u32[]{:S(2)}) collective-permute-start(f32[4,16,128]{2,1,0:T(8,128)S(1)} %fusion.85), channel_id=1, source_target_pairs={{0,1},{1,2},{2,3},{3,4},{4,5},{5,6},{6,7},{8,9},{9,10},{10,11},{11... | collective-permute-start | bytes 98312 | tf_op jit(solution)/shard_map/ppermute | solution.py:15
  240.4 5.0 %collective-permute-start.19 = (f32[4,16,128]{2,1,0:T(8,128)S(1)}, f32[4,16,128]{2,1,0:T(8,128)S(1)}, u32[]{:S(2)}, u32[]{:S(2)}) collective-permute-start(f32[4,16,128]{2,1,0:T(8,128)S(1)} %fusion.85), channel_id=1, source_target_pairs={{0,2},{1,3},{2,4},{3,5},{4,6},{5,7},{8,10},{9,11},{10,12},{11,13},... | collective-permute-start | bytes 98312 | tf_op jit(solution)/shard_map/ppermute | solution.py:15
  308.2 10.9 %collective-permute-start.24 = (f32[4,16,128]{2,1,0:T(8,128)S(1)}, f32[4,16,128]{2,1,0:T(8,128)S(1)}, u32[]{:S(2)}, u32[]{:S(2)}) collective-permute-start(f32[4,16,128]{2,1,0:T(8,128)S(1)} %fusion.3), channel_id=1, source_target_pairs={{0,3},{1,4},{2,5},{3,6},{4,7},{8,11},{9,12},{10,13},{11,14},{12,15... | collective-permute-start | bytes 98312 | tf_op jit(solution)/shard_map/ppermute | solution.py:15
  309.6 14.6 %collective-permute-start.29 = (f32[4,16,128]{2,1,0:T(8,128)S(1)}, f32[4,16,128]{2,1,0:T(8,128)S(1)}, u32[]{:S(2)}, u32[]{:S(2)}) collective-permute-start(f32[4,16,128]{2,1,0:T(8,128)S(1)} %fusion.3), channel_id=1, source_target_pairs={{3,0},{4,1},{5,2},{6,3},{7,4},{11,8},{12,9},{13,10},{14,11},{15,12... | collective-permute-start | bytes 98312 | tf_op jit(solution)/shard_map/ppermute | solution.py:15
  310.9 13.2 %collective-permute-start.28 = (f32[4,16,128]{2,1,0:T(8,128)S(1)}, f32[4,16,128]{2,1,0:T(8,128)S(1)}, u32[]{:S(2)}, u32[]{:S(2)}) collective-permute-start(f32[4,16,128]{2,1,0:T(8,128)S(1)} %fusion.3), channel_id=1, source_target_pairs={{2,0},{3,1},{4,2},{5,3},{6,4},{7,5},{10,8},{11,9},{12,10},{13,11},... | collective-permute-start | bytes 98312 | tf_op jit(solution)/shard_map/ppermute | solution.py:15
  312.2 11.9 %collective-permute-start.27 = (f32[4,16,128]{2,1,0:T(8,128)S(1)}, f32[4,16,128]{2,1,0:T(8,128)S(1)}, u32[]{:S(2)}, u32[]{:S(2)}) collective-permute-start(f32[4,16,128]{2,1,0:T(8,128)S(1)} %fusion.3), channel_id=1, source_target_pairs={{1,0},{2,1},{3,2},{4,3},{5,4},{6,5},{7,6},{9,8},{10,9},{11,10},{12... | collective-permute-start | bytes 98312 | tf_op jit(solution)/shard_map/ppermute | solution.py:15
  314.9 9.2 %collective-permute-start.26 = (f32[4,16,128]{2,1,0:T(8,128)S(1)}, f32[4,16,128]{2,1,0:T(8,128)S(1)}, u32[]{:S(2)}, u32[]{:S(2)}) collective-permute-start(f32[4,16,128]{2,1,0:T(8,128)S(1)} %fusion.3), channel_id=1, source_target_pairs={{0,1},{1,2},{2,3},{3,4},{4,5},{5,6},{6,7},{8,9},{9,10},{10,11},{11... | collective-permute-start | bytes 98312 | tf_op jit(solution)/shard_map/ppermute | solution.py:15
  319.1 5.0 %collective-permute-start.25 = (f32[4,16,128]{2,1,0:T(8,128)S(1)}, f32[4,16,128]{2,1,0:T(8,128)S(1)}, u32[]{:S(2)}, u32[]{:S(2)}) collective-permute-start(f32[4,16,128]{2,1,0:T(8,128)S(1)} %fusion.3), channel_id=1, source_target_pairs={{0,2},{1,3},{2,4},{3,5},{4,6},{5,7},{8,10},{9,11},{10,12},{11,13},... | collective-permute-start | bytes 98312 | tf_op jit(solution)/shard_map/ppermute | solution.py:15
  353.2 38.4 %copy-start.2 = (f32[4,16,128]{2,1,0:T(8,128)}, f32[4,16,128]{2,1,0:T(8,128)S(1)}, u32[]{:S(2)}) copy-start(f32[4,16,128]{2,1,0:T(8,128)S(1)} %fusion.2) | copy-start | bytes 98308
  353.3 18.6 %collective-permute-start.30 = (f32[4,16,128]{2,1,0:T(8,128)S(1)}, f32[4,16,128]{2,1,0:T(8,128)S(1)}, u32[]{:S(2)}, u32[]{:S(2)}) collective-permute-start(f32[4,16,128]{2,1,0:T(8,128)S(1)} %fusion.2), channel_id=1, source_target_pairs={{0,3},{1,4},{2,5},{3,6},{4,7},{5,8},{6,9},{7,10},{8,11},{9,12},{10... | collective-permute-start | bytes 98312 | tf_op jit(solution)/shard_map/ppermute | solution.py:15
  355.2 25.7 %collective-permute-start.35 = (f32[4,16,128]{2,1,0:T(8,128)S(1)}, f32[4,16,128]{2,1,0:T(8,128)S(1)}, u32[]{:S(2)}, u32[]{:S(2)}) collective-permute-start(f32[4,16,128]{2,1,0:T(8,128)S(1)} %fusion.2), channel_id=1, source_target_pairs={{3,0},{4,1},{5,2},{6,3},{7,4},{8,5},{9,6},{10,7},{11,8},{12,9},{13... | collective-permute-start | bytes 98312 | tf_op jit(solution)/shard_map/ppermute | solution.py:15
  362.4 18.4 %collective-permute-start.34 = (f32[4,16,128]{2,1,0:T(8,128)S(1)}, f32[4,16,128]{2,1,0:T(8,128)S(1)}, u32[]{:S(2)}, u32[]{:S(2)}) collective-permute-start(f32[4,16,128]{2,1,0:T(8,128)S(1)} %fusion.2), channel_id=1, source_target_pairs={{2,0},{3,1},{4,2},{5,3},{6,4},{7,5},{8,6},{9,7},{10,8},{11,9},{12,... | collective-permute-start | bytes 98312 | tf_op jit(solution)/shard_map/ppermute | solution.py:15
  364.4 16.4 %collective-permute-start.33 = (f32[4,16,128]{2,1,0:T(8,128)S(1)}, f32[4,16,128]{2,1,0:T(8,128)S(1)}, u32[]{:S(2)}, u32[]{:S(2)}) collective-permute-start(f32[4,16,128]{2,1,0:T(8,128)S(1)} %fusion.2), channel_id=1, source_target_pairs={{1,0},{2,1},{3,2},{4,3},{5,4},{6,5},{7,6},{8,7},{9,8},{10,9},{11,1... | collective-permute-start | bytes 98312 | tf_op jit(solution)/shard_map/ppermute | solution.py:15
  368.3 12.4 %collective-permute-start.32 = (f32[4,16,128]{2,1,0:T(8,128)S(1)}, f32[4,16,128]{2,1,0:T(8,128)S(1)}, u32[]{:S(2)}, u32[]{:S(2)}) collective-permute-start(f32[4,16,128]{2,1,0:T(8,128)S(1)} %fusion.2), channel_id=1, source_target_pairs={{0,1},{1,2},{2,3},{3,4},{4,5},{5,6},{6,7},{7,8},{8,9},{9,10},{10,1... | collective-permute-start | bytes 98312 | tf_op jit(solution)/shard_map/ppermute | solution.py:15
  371.9 8.9 %collective-permute-start.31 = (f32[4,16,128]{2,1,0:T(8,128)S(1)}, f32[4,16,128]{2,1,0:T(8,128)S(1)}, u32[]{:S(2)}, u32[]{:S(2)}) collective-permute-start(f32[4,16,128]{2,1,0:T(8,128)S(1)} %fusion.2), channel_id=1, source_target_pairs={{0,2},{1,3},{2,4},{3,5},{4,6},{5,7},{6,8},{7,9},{8,10},{9,11},{10,... | collective-permute-start | bytes 98312 | tf_op jit(solution)/shard_map/ppermute | solution.py:15
